TPU v7x, 32 devices: a whole 2x2x4 slice. The times are simulated.
32 devices in a mesh: slab: 8 (over y, x, core), grid: 4 (over z).
Axes of the slice: x: 2, y: 2, z: 4, core: 2. Of those that a mesh axis runs over, the one named last changes fastest.
Arguments:
- blocks: bfloat16 [8, 4, 16, 64, 4096], P('slab', 'grid')
- coords: int32 [8, 4, 16, 3], P('slab', 'grid'), may hold values from 0 to 15, as said below
- counts: int32 [8, 4], P('slab', 'grid'), may hold values from 2 to 16, as said below
- b_init: float32 [4096, 256], P(('slab', 'grid'))
- c_init: float32 [256, 256], replicated
Outputs:
- factor_a: float32 [8192, 256], P(('slab', 'grid'))
- factor_b: float32 [4096, 256], P(('slab', 'grid'))
- factor_c: float32 [256, 256], replicated
Inputs may be any that keep to these rules, and one draw needn't show every extreme that they name: `coords`: column 0 is below 16, column 1 below 16, column 2 below 4; the 16 slots of one device name different blocks. Slots 0 to counts - 1 of a device hold its blocks and the other slots are padding; at least one device uses all 16 slots.
All inputs are finite; a program needn't handle non-finite values.
Results may differ from a plain program's by a relative error of at most 0.0007.
The roundings to bfloat16 on the way count: a program that leaves them out, or rounds other values in their place, can miss the bound.
Values may be sent and summed in bfloat16 or wider, within the bound.
No kernel may reach another device: no remote copies, remote signals or barrier semaphores. Data moves between devices by JAX's collectives and lax.ppermute only.
A program may use at most 64 MiB of HBM per device.

v0:
```python
import functools

import jax
import jax.numpy as jnp
from jax import lax
from jax.experimental import pallas as pl
from jax.experimental.pallas import tpu as pltpu
from jax.sharding import PartitionSpec as P

W = 64
IBP = 16
JBP = 16
LANES = 128
PANEL = 128
GROUP = 4

HIGH = lax.Precision.HIGHEST
EPS = 1e-05
BOTH = ("slab", "grid")
F32 = jnp.float32
BF16 = jnp.bfloat16


def product_rows(first, second, start):
    rank = first.shape[1]
    pieces = []
    for row in range(start, start + GROUP):
        spread = jnp.broadcast_to(first[row : row + 1, :], (16, rank)).astype(BF16)
        pieces.append((second * spread[None]).reshape(W, rank))
    return jnp.concatenate(pieces, 0)


def slot_rows(coords_ref, slot, mode):
    return pl.multiple_of(coords_ref[slot * 3 + mode] * W, W)


def moments_kernel(mode, count_ref, coords_ref, blocks_ref, first_ref, second_ref, out_ref, *scratch):
    slot = pl.program_id(0)
    rank = out_ref.shape[1]

    @pl.when(slot == 0)
    def _():
        out_ref[...] = jnp.zeros_like(out_ref)

    spread_mode, tile_mode = ((1, 2), (0, 2), (1, 0))[mode]

    @pl.when(slot < count_ref[0])
    def _():
        first = first_ref[pl.ds(slot_rows(coords_ref, slot, spread_mode), W), :].astype(F32)
        second = second_ref[pl.ds(slot_rows(coords_ref, slot, tile_mode), W), :].reshape(4, 16, rank)
        target = slot_rows(coords_ref, slot, mode)
        total = jnp.zeros((W, rank), F32)
        if mode == 1:
            lanes_ref, order_ref = scratch
            columns = W * W // LANES
            for column in range(columns):
                lanes_ref[pl.ds(column, W, stride=columns), :] = blocks_ref[
                    0, :, column * LANES : (column + 1) * LANES
                ].astype(F32)
            low = lax.broadcasted_iota(jnp.int32, (columns, LANES), 1) < W
        for step in range(W // GROUP):
            right = product_rows(first, second, step * GROUP)
            if mode == 0:
                left = blocks_ref[0, :, step * GROUP * W : (step + 1) * GROUP * W]
            elif mode == 1:
                parts = []
                for pair in range(GROUP // 2):
                    row = step * GROUP + 2 * pair
                    one = lanes_ref[row * columns : (row + 1) * columns, :]
                    two = lanes_ref[(row + 1) * columns : (row + 2) * columns, :]
                    even = jnp.where(low, one, pltpu.roll(two, W, 1)).astype(BF16)
                    odd = jnp.where(low, pltpu.roll(one, W, 1), two).astype(BF16)
                    parts.append(jnp.concatenate([even, odd], 0))
                left = jnp.concatenate(parts, 1)
            else:
                parts = []
                for pair in range(GROUP // 2):
                    column = step * GROUP // 2 + pair
                    turned = blocks_ref[0, :, column * LANES : (column + 1) * LANES].T
                    parts += [turned[:W], turned[W:]]
                left = jnp.concatenate(parts, 1)
            total = total + jnp.dot(left, right, preferred_element_type=F32)
        if mode == 1:
            halves = []
            for part in range(rank // LANES):
                for parity in range(2):
                    order_ref[part, pl.ds(parity, W // 2, stride=2), :] = total[
                        parity * W // 2 : (parity + 1) * W // 2, part * LANES : (part + 1) * LANES
                    ]
                halves.append(order_ref[part])
            total = jnp.concatenate(halves, 1)
        out_ref[pl.ds(target, W), :] += total


def block_moments(mode, blocks, coords, count, first, second, out_rows):
    slots = blocks.shape[0]
    rank = first.shape[1]
    scratch = []
    if mode == 1:
        scratch = [
            pltpu.VMEM((W * W * W // LANES, LANES), F32),
            pltpu.VMEM((rank // LANES, W, LANES), F32),
        ]
    whole = lambda slot, count_ref, coords_ref: (0, 0)
    spec = pltpu.PrefetchScalarGridSpec(
        num_scalar_prefetch=2,
        grid=(slots,),
        in_specs=[
            pl.BlockSpec(
                (1, W, W * W),
                lambda slot, count_ref, coords_ref: (jnp.minimum(slot, count_ref[0] - 1), 0, 0),
            ),
            pl.BlockSpec(first.shape, whole),
            pl.BlockSpec(second.shape, whole),
        ],
        out_specs=pl.BlockSpec((out_rows, rank), whole),
        scratch_shapes=scratch,
    )
    return pl.pallas_call(
        functools.partial(moments_kernel, mode),
        grid_spec=spec,
        out_shape=jax.ShapeDtypeStruct((out_rows, rank), F32),
        compiler_params=pltpu.CompilerParams(vmem_limit_bytes=40 << 20),
        cost_estimate=pl.CostEstimate(
            flops=2 * slots * W**3 * rank, bytes_accessed=blocks.size * 2, transcendentals=0
        ),
    )(count, coords, blocks, first, second)


def exchange(rows, axes):
    devices = lax.axis_size(axes)
    parts = lax.all_to_all(rows, axes, split_axis=0, concat_axis=0, tiled=True)
    return parts.reshape(devices, rows.shape[0] // devices, rows.shape[1])


def spread_rows(rows, axes):
    devices = lax.axis_size(axes)
    return lax.all_to_all(jnp.tile(rows, (devices, 1)), axes, split_axis=0, concat_axis=0, tiled=True)


def total_sum(square):
    return spread_rows(jnp.sum(exchange(square, BOTH), axis=0), BOTH)


def gram_local(factor):
    return jnp.dot(factor.T, factor, precision=HIGH, preferred_element_type=F32)


def exact_dot(left, right, contract):
    return lax.dot_general(left, right, (contract, ((), ())), precision=HIGH, preferred_element_type=F32)


def across_lanes(tile, lane):
    return jnp.broadcast_to(tile[:, lane : lane + 1], tile.shape)


def across_rows(tile, row):
    return jnp.broadcast_to(tile[row : row + 1, :], tile.shape)


def tree_sum(terms):
    while len(terms) > 1:
        terms = [a + b for a, b in zip(terms[::2], terms[1::2])]
    return terms[0]


def sweep_corner(entries):
    for k in range(0, 8, 2):
        at = lambda i, j: entries[(min(i, j), max(i, j))]
        a, o, d = at(k, k), at(k, k + 1), at(k + 1, k + 1)
        inverse = 1.0 / (a * d - o * o)
        w00, w01, w11 = d * inverse, -(o * inverse), a * inverse
        rest = [j for j in range(8) if j not in (k, k + 1)]
        top = {j: w00 * at(k, j) + w01 * at(k + 1, j) for j in rest}
        low = {j: w01 * at(k, j) + w11 * at(k + 1, j) for j in rest}
        swept = {(k, k): -w00, (k, k + 1): -w01, (k + 1, k + 1): -w11}
        for i in rest:
            swept[(min(k, i), max(k, i))] = top[i]
            swept[(min(k + 1, i), max(k + 1, i))] = low[i]
            for j in rest:
                if i <= j:
                    swept[(i, j)] = at(i, j) - (at(k, i) * top[j] + at(k + 1, i) * low[j])
        entries = swept
    return entries


def panel_inverse(tiles):
    shape = tiles[0].shape
    lane = lax.broadcasted_iota(jnp.int32, shape, 1)
    row = lax.broadcasted_iota(jnp.int32, shape, 0)
    for pivot in range(len(tiles)):
        tile = tiles[pivot]
        first = 8 * pivot
        columns = [across_lanes(tile, first + j) for j in range(8)]
        corner = sweep_corner({(i, j): across_rows(columns[j], i) for j in range(8) for i in range(j + 1)})
        here = (lane >= first) & (lane < first + 8)
        turned = jnp.where(here, jnp.where(lane - first == row, 1.0, 0.0), -tile)
        rows = [across_rows(turned, i) for i in range(8)]
        scaled = [tree_sum([corner[(min(i, j), max(i, j))] * rows[j] for j in range(8)]) for i in range(8)]
        swept = []
        for other, held in enumerate(tiles):
            if other == pivot:
                mine = scaled[0]
                for i in range(1, 8):
                    mine = jnp.where(row == i, scaled[i], mine)
            else:
                change = tree_sum([across_lanes(held, first + j) * scaled[j] for j in range(8)])
                mine = jnp.where(here, 0.0, held) - change
            swept.append(mine)
        tiles = swept
    return -jnp.concatenate(tiles, 0)


def inverse_kernel(one_ref, two_ref, out_ref, held_ref):
    size = held_ref.shape[0]
    system = one_ref[...] * two_ref[...]
    shape = (size, size)
    on_diagonal = lax.broadcasted_iota(jnp.int32, shape, 0) == lax.broadcasted_iota(jnp.int32, shape, 1)
    diagonal = jnp.where(on_diagonal, system, 0.0)
    across = lax.rsqrt(jnp.sum(diagonal, 0, keepdims=True))
    down = lax.rsqrt(jnp.sum(diagonal, 1, keepdims=True))
    held_ref[...] = system * across * down
    here = lax.broadcasted_iota(jnp.int32, (1, size), 1) < PANEL
    rest = size - PANEL

    def eliminate(step, carry):
        pivot = panel_inverse([held_ref[8 * g : 8 * g + 8, :PANEL] for g in range(PANEL // 8)])
        rows = held_ref[:PANEL, :]
        scaled = exact_dot(pivot, rows, ((1,), (0,)))
        minus = jnp.concatenate([-pivot, jnp.zeros((PANEL, rest), F32)], 1)
        scaled = jnp.where(here, minus, scaled)
        others = jnp.where(here, 0.0, held_ref[PANEL:, :]) - exact_dot(
            rows[:, PANEL:], scaled, ((0,), (0,))
        )
        held_ref[:rest, :] = pltpu.roll(others, rest, 1)
        held_ref[rest:, :] = pltpu.roll(scaled, rest, 1)
        return carry

    lax.fori_loop(0, size // PANEL, eliminate, 0)
    out_ref[...] = -held_ref[...] * across * down


def product_inverse(one, two):
    return pl.pallas_call(
        inverse_kernel,
        out_shape=jax.ShapeDtypeStruct(one.shape, F32),
        scratch_shapes=[pltpu.VMEM(one.shape, F32)],
        compiler_params=pltpu.CompilerParams(vmem_limit_bytes=16 << 20),
        cost_estimate=pl.CostEstimate(flops=6 * one.shape[0] ** 3 * 40, bytes_accessed=3 * one.size * 4, transcendentals=0),
    )(one, two)


def solve_kernel(parts_ref, inverse_ref, raw_ref, *gram_ref):
    moments = parts_ref[0]
    for part in range(1, parts_ref.shape[0]):
        moments = moments + parts_ref[part]
    raw = exact_dot(moments, inverse_ref[...], ((1,), (0,)))
    raw_ref[...] = raw
    if gram_ref:
        gram_ref[0][...] = exact_dot(raw, raw, ((0,), (0,)))


def solve_rows(parts, inverse, with_gram):
    rows, rank = parts.shape[1:]
    out_shape = [jax.ShapeDtypeStruct((rows, rank), F32)]
    if with_gram:
        out_shape.append(jax.ShapeDtypeStruct((rank, rank), F32))
    return pl.pallas_call(
        solve_kernel,
        out_shape=out_shape,
        compiler_params=pltpu.CompilerParams(vmem_limit_bytes=16 << 20),
    )(parts, inverse)


def scale_kernel(row_total, total_ref, raw_ref, factor_ref, rounded_ref, gram_ref):
    mean = total_ref[...] / row_total
    shape = mean.shape
    on_diagonal = lax.broadcasted_iota(jnp.int32, shape, 0) == lax.broadcasted_iota(jnp.int32, shape, 1)
    diagonal = jnp.where(on_diagonal, mean, 0.0)
    across = jnp.sqrt(jnp.sum(diagonal, 0, keepdims=True) + EPS)
    down = jnp.sqrt(jnp.sum(diagonal, 1, keepdims=True) + EPS)
    gram_ref[...] = mean / across / down
    factor = raw_ref[...] / across
    factor_ref[...] = factor
    rounded_ref[...] = factor.astype(BF16)


def scale_rows(gram_total, raw, row_total):
    return pl.pallas_call(
        functools.partial(scale_kernel, row_total),
        out_shape=[
            jax.ShapeDtypeStruct(raw.shape, F32),
            jax.ShapeDtypeStruct(raw.shape, BF16),
            jax.ShapeDtypeStruct(gram_total.shape, F32),
        ],
        compiler_params=pltpu.CompilerParams(vmem_limit_bytes=16 << 20),
    )(gram_total, raw)


def on_device(blocks, coords, counts, b_init, c_init):
    slab_count = lax.axis_size("slab")
    grid_count = lax.axis_size("grid")
    local_blocks = blocks[0, 0]
    local_coords = coords.reshape(-1)
    filled = counts.reshape(-1)
    doc_rows = IBP * W
    term_rows = JBP * W
    doc_total = doc_rows * slab_count
    term_total = term_rows * grid_count
    month_total = c_init.shape[0]
    month_bf = c_init.astype(BF16)
    gram_c = gram_local(c_init) / month_total
    gram_b = total_sum(gram_local(b_init)) / term_total
    term_panel = lax.all_gather(b_init.astype(BF16), "slab", axis=0, tiled=True)
    moments_a = block_moments(0, local_blocks, local_coords, filled, term_panel, month_bf, doc_rows)
    parts_a = exchange(moments_a, "grid")
    inverse_a = product_inverse(gram_b, gram_c)
    raw_a, own_gram_a = solve_rows(parts_a, inverse_a, True)
    factor_a, rounded_a, gram_a = scale_rows(total_sum(own_gram_a), raw_a, doc_total)
    doc_panel = lax.all_gather(rounded_a, "grid", axis=0, tiled=True)
    moments_b = block_moments(1, local_blocks, local_coords, filled, doc_panel, month_bf, term_rows)
    parts_b = exchange(moments_b, "slab")
    inverse_b = product_inverse(gram_a, gram_c)
    raw_b, own_gram_b = solve_rows(parts_b, inverse_b, True)
    factor_b, rounded_b, gram_bn = scale_rows(total_sum(own_gram_b), raw_b, term_total)
    term_panel_new = lax.all_gather(rounded_b, "slab", axis=0, tiled=True)
    moments_c = block_moments(
        2, local_blocks, local_coords, filled, term_panel_new, doc_panel, month_total
    )
    parts_c = exchange(moments_c, BOTH)
    inverse_c = product_inverse(gram_a, gram_bn)
    (raw_own,) = solve_rows(parts_c, inverse_c, False)
    raw_c = spread_rows(raw_own, BOTH)
    column_scale = jnp.sqrt(jnp.mean(raw_c * raw_c, axis=0) + EPS)
    return (factor_a, factor_b, raw_c / column_scale)


def solution(mesh):
    in_specs = (
        P("slab", "grid", None, None, None),
        P("slab", "grid", None, None),
        P("slab", "grid"),
        P(("slab", "grid"), None),
        P(),
    )
    out_specs = (P(("slab", "grid"), None), P(("slab", "grid"), None), P())
    return jax.shard_map(
        on_device, mesh=mesh, in_specs=in_specs, out_specs=out_specs, check_vma=False
    )
```

profile of v0, /device:TPU:0, one launch (start us, length us, event | category | flops | bytes accessed | tf_op | source)
XLA Modules:
  0.0 242.4 jit_solution(16227742351231533975)
XLA Ops:
  0.6 0.0 copy-start.3
  0.6 1.4 convolution_bitcast_fusion
  2.1 17.3 %all_to_all.85 = f32[32,8,256]{2,1,0:T(8,128)S(1)} all-to-all(f32[32,8,256]{2,1,0:T(8,128)S(1)} %convolution_bitcast_fusion), channel_id=1, replica_groups=mesh['slab'=8,'grid'=4] {'slab','grid'}, dimensions={0} | all-to-all | bytes 524288 | tf_op jit(solution)/shard_map/all_to_all | solution.py:132
  19.4 0.7 tile.8
  20.1 2.7 %all-to-all-start.2 = ((f32[32,8,256]{2,1,0:T(8,128)}), f32[32,8,256]{2,1,0:T(8,128)S(1)}, u32[]{:S(2)}, u32[]{:S(2)}) async-start(f32[32,8,256]{2,1,0:T(8,128)} %tile.8), calls=%async_computation.2 | async-start | bytes 524288 | tf_op jit(solution)/shard_map/all_to_all | solution.py:138
  22.9 0.9 convert_element_type.6
  24.4 0.8 copy.9
  25.2 0.1 reshape.72.coords_ref
  25.3 1.0 convert_element_type.7.second_ref
  26.3 10.3 %all_gather.9.first_ref = bf16[1024,256]{1,0:T(8,128)(2,1)S(1)} all-gather(bf16[128,256]{1,0:T(8,128)(2,1)S(1)} %convert_element_type.6), channel_id=1, replica_groups=mesh['slab'=8,'grid'=4] {'slab'}, dimensions={0}, use_global_device_ids=true | all-gather | bytes 589824 | tf_op jit(solution)/shard_map/all_gather | solution.py:314
  36.5 0.0 copy-start
  36.5 3.4 %copy-done = bf16[1,1,16,64,4096]{4,3,2,1,0:T(8,128)(2,1)S(1)} copy-done((bf16[1,1,16,64,4096]{4,3,2,1,0:T(8,128)(2,1)S(1)}, bf16[1,1,16,64,4096]{4,3,2,1,0:T(8,128)(2,1)}, u32[]{:S(2)}) %copy-start) | copy-done | bytes 8388632
  39.9 4.9 %shard_map.76 = f32[1024,256]{1,0:T(8,128)} custom-call(s32[1]{0:T(128)} %bitcast.21.count_ref, s32[48]{0:T(128)S(1)} %reshape.72.coords_ref, bf16[16,64,4096]{2,1,0:T(8,128)(2,1)S(1)} %bitcast.24, bf16[1024,256]{1,0:T(8,128)(2,1)S(1)} %all_gather.9.first_ref, bf16[256,256]{1,0:T(8,128)(2,1)S(1)} %convert_element_type.7.second_ref), custom_call_target="tpu_custom_call" | custom-call | flops 2147483648 | bytes 8388608 | tf_op jit(solution)/shard_map/pallas_call | solution.py:119
  44.9 0.0 all-to-all-done.2
  44.9 3.5 %all-to-all-start = ((f32[4,256,256]{2,1,0:T(8,128)}), f32[4,256,256]{2,1,0:T(8,128)S(1)}, u32[]{:S(2)}, u32[]{:S(2)}) async-start(f32[4,256,256]{2,1,0:T(8,128)} %bitcast.2), calls=%async_computation | async-start | bytes 2097152 | tf_op jit(solution)/shard_map/all_to_all | solution.py:132
  48.4 0.0 copy-done.3
  48.4 0.6 convolution_multiply_fusion.two_ref
  49.0 10.8 %shard_map.77.inverse_ref = f32[256,256]{1,0:T(8,128)S(1)} custom-call(f32[256,256]{1,0:T(8,128)S(1)} %multiply_bitcast_fusion.one_ref, f32[256,256]{1,0:T(8,128)S(1)} %convolution_multiply_fusion.two_ref), custom_call_target="tpu_custom_call" | custom-call | flops 4026531840 | bytes 786432 | tf_op jit(solution)/shard_map/pallas_call | solution.py:244
  59.8 15.4 %all-to-all-done.parts_ref = f32[4,256,256]{2,1,0:T(8,128)S(1)} async-done(((f32[4,256,256]{2,1,0:T(8,128)}), f32[4,256,256]{2,1,0:T(8,128)S(1)}, u32[]{:S(2)}, u32[]{:S(2)}) %all-to-all-start) | async-done | bytes 1048608 | tf_op jit(solution)/shard_map/all_to_all | solution.py:132
  75.2 1.1 shard_map.78
  76.4 13.6 %all_to_all.86 = f32[32,8,256]{2,1,0:T(8,128)S(1)} all-to-all(f32[32,8,256]{2,1,0:T(8,128)S(1)} %bitcast.29), channel_id=1, replica_groups=mesh['slab'=8,'grid'=4] {'slab','grid'}, dimensions={0} | all-to-all | bytes 524288 | tf_op jit(solution)/shard_map/all_to_all | solution.py:132
  90.0 12.7 %all_to_all.87 = f32[32,8,256]{2,1,0:T(8,128)S(1)} all-to-all(f32[32,8,256]{2,1,0:T(8,128)S(1)} %tile.9), channel_id=1, replica_groups=mesh['slab'=8,'grid'=4] {'slab','grid'}, dimensions={0} | all-to-all | bytes 524288 | tf_op jit(solution)/shard_map/all_to_all | solution.py:138
  102.7 0.8 shard_map.79
  103.5 16.1 %all_gather.10.first_ref.second_ref = bf16[1024,256]{1,0:T(8,128)(2,1)S(1)} all-gather(bf16[256,256]{1,0:T(8,128)(2,1)S(1)} %get-tuple-element.16), channel_id=1, replica_groups=mesh['slab'=8,'grid'=4] {'grid'}, dimensions={0}, use_global_device_ids=true | all-gather | bytes 655360 | tf_op jit(solution)/shard_map/all_gather | solution.py:320
  119.7 0.0 copy-start.1
  119.7 3.4 %copy-done.1 = bf16[1,1,16,64,4096]{4,3,2,1,0:T(8,128)(2,1)S(1)} copy-done((bf16[1,1,16,64,4096]{4,3,2,1,0:T(8,128)(2,1)S(1)}, bf16[1,1,16,64,4096]{4,3,2,1,0:T(8,128)(2,1)}, u32[]{:S(2)}) %copy-start.1) | copy-done | bytes 8388632
  123.1 8.3 %shard_map.80 = f32[1024,256]{1,0:T(8,128)} custom-call(s32[1]{0:T(128)} %bitcast.22.count_ref, s32[48]{0:T(128)S(1)} %reshape.72.coords_ref, bf16[16,64,4096]{2,1,0:T(8,128)(2,1)S(1)} %bitcast.25, bf16[1024,256]{1,0:T(8,128)(2,1)S(1)} %all_gather.10.first_ref.second_ref, bf16[256,256]{1,0:T(8,128)(2,1)S(1)} %convert_element_type.7.second_ref), custom_call_target="tpu_custom_call" | custom-call | flops 2147483648 | bytes 8388608 | tf_op jit(solution)/shard_map/pallas_call | solution.py:119
  131.4 4.3 %all-to-all-start.5 = ((f32[8,128,256]{2,1,0:T(8,128)}), f32[8,128,256]{2,1,0:T(8,128)S(1)}, u32[]{:S(2)}, u32[]{:S(2)}) async-start(f32[8,128,256]{2,1,0:T(8,128)} %bitcast.7), calls=%async_computation.5 | async-start | bytes 2097152 | tf_op jit(solution)/shard_map/all_to_all | solution.py:132
  135.7 10.8 %shard_map.81.inverse_ref = f32[256,256]{1,0:T(8,128)S(1)} custom-call(f32[256,256]{1,0:T(8,128)S(1)} %get-tuple-element.17.one_ref, f32[256,256]{1,0:T(8,128)S(1)} %convolution_multiply_fusion.two_ref), custom_call_target="tpu_custom_call" | custom-call | flops 4026531840 | bytes 786432 | tf_op jit(solution)/shard_map/pallas_call | solution.py:244
  146.5 4.6 %all-to-all-done.5.parts_ref = f32[8,128,256]{2,1,0:T(8,128)S(1)} async-done(((f32[8,128,256]{2,1,0:T(8,128)}), f32[8,128,256]{2,1,0:T(8,128)S(1)}, u32[]{:S(2)}, u32[]{:S(2)}) %all-to-all-start.5) | async-done | bytes 1048608 | tf_op jit(solution)/shard_map/all_to_all | solution.py:132
  151.1 0.9 shard_map.82
  152.0 19.6 %all_to_all.88 = f32[32,8,256]{2,1,0:T(8,128)S(1)} all-to-all(f32[32,8,256]{2,1,0:T(8,128)S(1)} %bitcast.30), channel_id=1, replica_groups=mesh['slab'=8,'grid'=4] {'slab','grid'}, dimensions={0} | all-to-all | bytes 524288 | tf_op jit(solution)/shard_map/all_to_all | solution.py:132
  171.7 12.7 %all_to_all.89 = f32[32,8,256]{2,1,0:T(8,128)S(1)} all-to-all(f32[32,8,256]{2,1,0:T(8,128)S(1)} %tile.10), channel_id=1, replica_groups=mesh['slab'=8,'grid'=4] {'slab','grid'}, dimensions={0} | all-to-all | bytes 524288 | tf_op jit(solution)/shard_map/all_to_all | solution.py:138
  184.4 0.7 shard_map.83
  185.1 9.4 %all_gather.11.first_ref = bf16[1024,256]{1,0:T(8,128)(2,1)S(1)} all-gather(bf16[128,256]{1,0:T(8,128)(2,1)S(1)} %get-tuple-element.21), channel_id=1, replica_groups=mesh['slab'=8,'grid'=4] {'slab'}, dimensions={0}, use_global_device_ids=true | all-gather | bytes 589824 | tf_op jit(solution)/shard_map/all_gather | solution.py:326
  194.5 0.0 copy-start.2
  194.5 3.4 %copy-done.2 = bf16[1,1,16,64,4096]{4,3,2,1,0:T(8,128)(2,1)S(1)} copy-done((bf16[1,1,16,64,4096]{4,3,2,1,0:T(8,128)(2,1)S(1)}, bf16[1,1,16,64,4096]{4,3,2,1,0:T(8,128)(2,1)}, u32[]{:S(2)}) %copy-start.2) | copy-done | bytes 8388632
  197.9 6.8 %shard_map.84 = f32[256,256]{1,0:T(8,128)} custom-call(s32[1]{0:T(128)} %bitcast.23.count_ref, s32[48]{0:T(128)S(1)} %reshape.72.coords_ref, bf16[16,64,4096]{2,1,0:T(8,128)(2,1)S(1)} %bitcast.26, bf16[1024,256]{1,0:T(8,128)(2,1)S(1)} %all_gather.11.first_ref, bf16[1024,256]{1,0:T(8,128)(2,1)S(1)} %all_gather.10.first_ref.second_ref), custom_call_target="tpu_custom_call" | custom-call | flops 2147483648 | bytes 8388608 | tf_op jit(solution)/shard_map/pallas_call | solution.py:119
  204.7 10.2 %all-to-all-start.8 = ((f32[32,8,256]{2,1,0:T(8,128)}), f32[32,8,256]{2,1,0:T(8,128)S(1)}, u32[]{:S(2)}, u32[]{:S(2)}) async-start(f32[32,8,256]{2,1,0:T(8,128)} %bitcast.10), calls=%async_computation.8 | async-start | bytes 524288 | tf_op jit(solution)/shard_map/all_to_all | solution.py:132
  214.9 10.8 %shard_map.85.inverse_ref = f32[256,256]{1,0:T(8,128)S(1)} custom-call(f32[256,256]{1,0:T(8,128)S(1)} %get-tuple-element.17.one_ref, f32[256,256]{1,0:T(8,128)S(1)} %get-tuple-element.22.two_ref), custom_call_target="tpu_custom_call" | custom-call | flops 4026531840 | bytes 786432 | tf_op jit(solution)/shard_map/pallas_call | solution.py:244
  225.7 0.0 all-to-all-done.8.parts_ref
  225.7 0.2 shard_map.86
  225.9 15.6 %all_to_all.90 = f32[32,8,256]{2,1,0:T(8,128)S(1)} all-to-all(f32[32,8,256]{2,1,0:T(8,128)S(1)} %tile.11), channel_id=1, replica_groups=mesh['slab'=8,'grid'=4] {'slab','grid'}, dimensions={0} | all-to-all | bytes 524288 | tf_op jit(solution)/shard_map/all_to_all | solution.py:138
  241.6 0.7 bitcast_divide_fusion
  (9 shorter events, 0.3 us)
Async XLA Ops:
  0.6 47.8 %copy-start.3 = (f32[256,256]{1,0:T(8,128)S(1)}, f32[256,256]{1,0:T(8,128)}, u32[]{:S(2)}) copy-start(f32[256,256]{1,0:T(8,128)} %param.9) | copy-start | bytes 786436
  20.1 24.7 %all-to-all-start.2 = ((f32[32,8,256]{2,1,0:T(8,128)}), f32[32,8,256]{2,1,0:T(8,128)S(1)}, u32[]{:S(2)}, u32[]{:S(2)}) async-start(f32[32,8,256]{2,1,0:T(8,128)} %tile.8), calls=%async_computation.2 | async-start | bytes 524288 | tf_op jit(solution)/shard_map/all_to_all | solution.py:138
  36.5 3.4 %copy-start = (bf16[1,1,16,64,4096]{4,3,2,1,0:T(8,128)(2,1)S(1)}, bf16[1,1,16,64,4096]{4,3,2,1,0:T(8,128)(2,1)}, u32[]{:S(2)}) copy-start(bf16[1,1,16,64,4096]{4,3,2,1,0:T(8,128)(2,1)} %param.5) | copy-start | bytes 25165828
  44.9 30.4 %all-to-all-start = ((f32[4,256,256]{2,1,0:T(8,128)}), f32[4,256,256]{2,1,0:T(8,128)S(1)}, u32[]{:S(2)}, u32[]{:S(2)}) async-start(f32[4,256,256]{2,1,0:T(8,128)} %bitcast.2), calls=%async_computation | async-start | bytes 2097152 | tf_op jit(solution)/shard_map/all_to_all | solution.py:132
  119.7 3.4 %copy-start.1 = (bf16[1,1,16,64,4096]{4,3,2,1,0:T(8,128)(2,1)S(1)}, bf16[1,1,16,64,4096]{4,3,2,1,0:T(8,128)(2,1)}, u32[]{:S(2)}) copy-start(bf16[1,1,16,64,4096]{4,3,2,1,0:T(8,128)(2,1)} %param.5) | copy-start | bytes 25165828
  131.4 19.7 %all-to-all-start.5 = ((f32[8,128,256]{2,1,0:T(8,128)}), f32[8,128,256]{2,1,0:T(8,128)S(1)}, u32[]{:S(2)}, u32[]{:S(2)}) async-start(f32[8,128,256]{2,1,0:T(8,128)} %bitcast.7), calls=%async_computation.5 | async-start | bytes 2097152 | tf_op jit(solution)/shard_map/all_to_all | solution.py:132
  194.5 3.4 %copy-start.2 = (bf16[1,1,16,64,4096]{4,3,2,1,0:T(8,128)(2,1)S(1)}, bf16[1,1,16,64,4096]{4,3,2,1,0:T(8,128)(2,1)}, u32[]{:S(2)}) copy-start(bf16[1,1,16,64,4096]{4,3,2,1,0:T(8,128)(2,1)} %param.5) | copy-start | bytes 25165828
  204.7 21.0 %all-to-all-start.8 = ((f32[32,8,256]{2,1,0:T(8,128)}), f32[32,8,256]{2,1,0:T(8,128)S(1)}, u32[]{:S(2)}, u32[]{:S(2)}) async-start(f32[32,8,256]{2,1,0:T(8,128)} %bitcast.10), calls=%async_computation.8 | async-start | bytes 524288 | tf_op jit(solution)/shard_map/all_to_all | solution.py:132
where the time goes:
time: 240 us; the launch traced here: 242 us
  blocking collectives  127 us (53%)
  Pallas kernels  56.1 us (23%)
  starting transfers between devices  20.7 us (9%)
  waiting for transfers between devices  20 us (8%)
  local copies, waits for them, and re-layouts  11.8 us (5%)
  other arithmetic  2.8 us (1%)
    all_to_all x3, blocking collectives, exchange(): parts = lax.all_to_all(rows, axes, split_axis=0, concat_axis=0, tiled=True)  50.5 us
    all_to_all x3, blocking collectives, spread_rows(): lax.all_to_all(jnp.tile(rows, (devices, 1)), axes, split_axis=0, concat_a...  41.1 us
    pallas_call x3, Pallas kernels, product_inverse(): pl.pallas_call(inverse_kernel, out_shape=jax.ShapeDtypeStruct(one.shape,...  32.4 us
    pallas_call x3, Pallas kernels, block_moments(): pl.pallas_call(functools.partial(moments_kernel, mode), grid_spec=spec, o...  20 us
    all_to_all x3, waiting for transfers between devices, exchange(): parts = lax.all_to_all(rows, axes, split_axis=0, concat_axis=0, tiled=True)  20 us
    all_to_all x3, starting transfers between devices, exchange(): parts = lax.all_to_all(rows, axes, split_axis=0, concat_axis=0, tiled=True)  18 us
    all_gather x1, blocking collectives, on_device(): doc_panel = lax.all_gather(rounded_a, 'grid', axis=0, tiled=True)  16.1 us
    unnamed x9, local copies, waits for them, and re-layouts  10.9 us
  transfers between devices with their start and end apart: 4, of which 2 were waited for; matrix products, arithmetic and copies ran while one was open for 1% of the time, Pallas kernels for 15%

commit v1 on v0

--- a/solution.py
+++ b/solution.py
@@ -30,11 +30,15 @@
     return jnp.concatenate(pieces, 0)
 
 
-def slot_rows(coords_ref, slot, mode):
-    return pl.multiple_of(coords_ref[slot * 3 + mode] * W, W)
-
-
-def moments_kernel(mode, count_ref, coords_ref, blocks_ref, first_ref, second_ref, out_ref, *scratch):
+def slot_rows(coords_ref, slot, mode, order):
+    block = coords_ref[slot * 3 + mode]
+    if order is not None:
+        each = IBP // lax.axis_size(order)
+        block = ((block // each) ^ lax.axis_index(order)) * each + block % each
+    return pl.multiple_of(block * W, W)
+
+
+def moments_kernel(mode, orders, count_ref, coords_ref, blocks_ref, first_ref, second_ref, out_ref, *scratch):
     slot = pl.program_id(0)
     rank = out_ref.shape[1]
 
@@ -46,9 +50,9 @@
 
     @pl.when(slot < count_ref[0])
     def _():
-        first = first_ref[pl.ds(slot_rows(coords_ref, slot, spread_mode), W), :].astype(F32)
-        second = second_ref[pl.ds(slot_rows(coords_ref, slot, tile_mode), W), :].reshape(4, 16, rank)
-        target = slot_rows(coords_ref, slot, mode)
+        first = first_ref[pl.ds(slot_rows(coords_ref, slot, spread_mode, orders[0]), W), :].astype(F32)
+        second = second_ref[pl.ds(slot_rows(coords_ref, slot, tile_mode, orders[1]), W), :].reshape(4, 16, rank)
+        target = slot_rows(coords_ref, slot, mode, orders[2])
         total = jnp.zeros((W, rank), F32)
         if mode == 1:
             lanes_ref, order_ref = scratch
@@ -92,7 +96,7 @@
         out_ref[pl.ds(target, W), :] += total
 
 
-def block_moments(mode, blocks, coords, count, first, second, out_rows):
+def block_moments(mode, orders, blocks, coords, count, first, second, out_rows):
     slots = blocks.shape[0]
     rank = first.shape[1]
     scratch = []
@@ -117,10 +121,10 @@
         scratch_shapes=scratch,
     )
     return pl.pallas_call(
-        functools.partial(moments_kernel, mode),
+        functools.partial(moments_kernel, mode, orders),
         grid_spec=spec,
         out_shape=jax.ShapeDtypeStruct((out_rows, rank), F32),
-        compiler_params=pltpu.CompilerParams(vmem_limit_bytes=40 << 20),
+        compiler_params=pltpu.CompilerParams(vmem_limit_bytes=14 << 20),
         cost_estimate=pl.CostEstimate(
             flops=2 * slots * W**3 * rank, bytes_accessed=blocks.size * 2, transcendentals=0
         ),
@@ -140,6 +144,20 @@
 
 def total_sum(square):
     return spread_rows(jnp.sum(exchange(square, BOTH), axis=0), BOTH)
+
+
+def swap(rows, axis, step):
+    return lax.ppermute(rows, axis, [(i, i ^ step) for i in range(lax.axis_size(axis))])
+
+
+def swap_pieces(rows, axis):
+    devices = lax.axis_size(axis)
+    each = rows.shape[0] // devices
+    return [swap(rows[k * each : (k + 1) * each], axis, k) for k in range(1, devices)]
+
+
+def swap_gather(rows, axis):
+    return jnp.concatenate([rows] + [swap(rows, axis, k) for k in range(1, lax.axis_size(axis))], 0)
 
 
 def gram_local(factor):
@@ -211,14 +229,25 @@
     return -jnp.concatenate(tiles, 0)
 
 
-def inverse_kernel(one_ref, two_ref, out_ref, held_ref):
+def on_diagonal(size):
+    shape = (size, size)
+    return lax.broadcasted_iota(jnp.int32, shape, 0) == lax.broadcasted_iota(jnp.int32, shape, 1)
+
+
+def turned_down(across, diagonal):
+    return jnp.sum(jnp.where(diagonal, across, 0.0), 1, keepdims=True)
+
+
+def inverse_kernel(totals, one_ref, one_scale_ref, two_ref, two_scale_ref, out_ref, held_ref):
     size = held_ref.shape[0]
-    system = one_ref[...] * two_ref[...]
-    shape = (size, size)
-    on_diagonal = lax.broadcasted_iota(jnp.int32, shape, 0) == lax.broadcasted_iota(jnp.int32, shape, 1)
-    diagonal = jnp.where(on_diagonal, system, 0.0)
-    across = lax.rsqrt(jnp.sum(diagonal, 0, keepdims=True))
-    down = lax.rsqrt(jnp.sum(diagonal, 1, keepdims=True))
+    diagonal = on_diagonal(size)
+    system = None
+    for total, gram_ref, scale_ref in zip(totals, (one_ref, two_ref), (one_scale_ref, two_scale_ref)):
+        inverse_scale = 1.0 / scale_ref[...]
+        gram = gram_ref[...] * (inverse_scale / total) * turned_down(inverse_scale, diagonal)
+        system = gram if system is None else system * gram
+    across = lax.rsqrt(jnp.sum(jnp.where(diagonal, system, 0.0), 0, keepdims=True))
+    down = turned_down(across, diagonal)
     held_ref[...] = system * across * down
     here = lax.broadcasted_iota(jnp.int32, (1, size), 1) < PANEL
     rest = size - PANEL
@@ -241,60 +270,73 @@
 
 
 def product_inverse(one, two):
+    shape = one[0].shape
     return pl.pallas_call(
-        inverse_kernel,
-        out_shape=jax.ShapeDtypeStruct(one.shape, F32),
-        scratch_shapes=[pltpu.VMEM(one.shape, F32)],
-        compiler_params=pltpu.CompilerParams(vmem_limit_bytes=16 << 20),
-        cost_estimate=pl.CostEstimate(flops=6 * one.shape[0] ** 3 * 40, bytes_accessed=3 * one.size * 4, transcendentals=0),
-    )(one, two)
-
-
-def solve_kernel(parts_ref, inverse_ref, raw_ref, *gram_ref):
-    moments = parts_ref[0]
-    for part in range(1, parts_ref.shape[0]):
-        moments = moments + parts_ref[part]
-    raw = exact_dot(moments, inverse_ref[...], ((1,), (0,)))
-    raw_ref[...] = raw
-    if gram_ref:
-        gram_ref[0][...] = exact_dot(raw, raw, ((0,), (0,)))
-
-
-def solve_rows(parts, inverse, with_gram):
-    rows, rank = parts.shape[1:]
-    out_shape = [jax.ShapeDtypeStruct((rows, rank), F32)]
-    if with_gram:
-        out_shape.append(jax.ShapeDtypeStruct((rank, rank), F32))
+        functools.partial(inverse_kernel, (one[1], two[1])),
+        out_shape=jax.ShapeDtypeStruct(shape, F32),
+        scratch_shapes=[pltpu.VMEM(shape, F32)],
+        compiler_params=pltpu.CompilerParams(vmem_limit_bytes=10 << 20),
+        cost_estimate=pl.CostEstimate(flops=10**10, bytes_accessed=3 << 18, transcendentals=0),
+    )(one[0], one[2], two[0], two[2])
+
+
+def solve_kernel(stacked, parts, *refs):
+    inverse_ref, outs = refs[parts], refs[parts + 1 :]
+    if stacked:
+        terms = [refs[0][part] for part in range(refs[0].shape[0])]
+    else:
+        terms = [ref[...] for ref in refs[:parts]]
+    raw = exact_dot(functools.reduce(jnp.add, terms), inverse_ref[...], ((1,), (0,)))
+    outs[0][...] = raw
+    if len(outs) > 1:
+        outs[1][...] = exact_dot(raw, raw, ((0,), (0,)))
+        outs[2][...] = jnp.broadcast_to(jnp.sum(raw * raw, 0, keepdims=True), outs[2].shape)
+
+
+def solve_swapped(own, others, inverse, devices):
+    rows, rank = others[0].shape
+    whole = pl.BlockSpec((rows, rank), lambda step: (0, 0))
+    square = pl.BlockSpec((rank, rank), lambda step: (0, 0))
     return pl.pallas_call(
-        solve_kernel,
-        out_shape=out_shape,
-        compiler_params=pltpu.CompilerParams(vmem_limit_bytes=16 << 20),
-    )(parts, inverse)
-
-
-def scale_kernel(row_total, total_ref, raw_ref, factor_ref, rounded_ref, gram_ref):
-    mean = total_ref[...] / row_total
-    shape = mean.shape
-    on_diagonal = lax.broadcasted_iota(jnp.int32, shape, 0) == lax.broadcasted_iota(jnp.int32, shape, 1)
-    diagonal = jnp.where(on_diagonal, mean, 0.0)
-    across = jnp.sqrt(jnp.sum(diagonal, 0, keepdims=True) + EPS)
-    down = jnp.sqrt(jnp.sum(diagonal, 1, keepdims=True) + EPS)
-    gram_ref[...] = mean / across / down
-    factor = raw_ref[...] / across
+        functools.partial(solve_kernel, False, 1 + len(others)),
+        grid=(1,),
+        in_specs=[whole] * (1 + len(others)) + [square],
+        out_specs=[whole, square, pl.BlockSpec((devices, rank), lambda step: (0, 0))],
+        out_shape=[
+            jax.ShapeDtypeStruct((rows, rank), F32),
+            jax.ShapeDtypeStruct((rank, rank), F32),
+            jax.ShapeDtypeStruct((devices, rank), F32),
+        ],
+        compiler_params=pltpu.CompilerParams(vmem_limit_bytes=10 << 20),
+    )(own, *others, inverse)
+
+
+def solve_stacked(parts, inverse):
+    return pl.pallas_call(
+        functools.partial(solve_kernel, True, 1),
+        out_shape=[jax.ShapeDtypeStruct(parts.shape[1:], F32)],
+        compiler_params=pltpu.CompilerParams(vmem_limit_bytes=10 << 20),
+    )(parts, inverse)[0]
+
+
+def scale_kernel(row_total, squares_ref, raw_ref, factor_ref, rounded_ref, scale_ref):
+    scale = jnp.sqrt(jnp.sum(squares_ref[...], 0, keepdims=True) / row_total + EPS)
+    scale_ref[...] = scale
+    factor = raw_ref[...] / scale
     factor_ref[...] = factor
     rounded_ref[...] = factor.astype(BF16)
 
 
-def scale_rows(gram_total, raw, row_total):
+def scale_rows(squares, raw, row_total):
     return pl.pallas_call(
         functools.partial(scale_kernel, row_total),
         out_shape=[
             jax.ShapeDtypeStruct(raw.shape, F32),
             jax.ShapeDtypeStruct(raw.shape, BF16),
-            jax.ShapeDtypeStruct(gram_total.shape, F32),
+            jax.ShapeDtypeStruct((1, raw.shape[1]), F32),
         ],
-        compiler_params=pltpu.CompilerParams(vmem_limit_bytes=16 << 20),
-    )(gram_total, raw)
+        compiler_params=pltpu.CompilerParams(vmem_limit_bytes=10 << 20),
+    )(squares, raw)
 
 
 def on_device(blocks, coords, counts, b_init, c_init):
@@ -309,28 +351,43 @@
     term_total = term_rows * grid_count
     month_total = c_init.shape[0]
     month_bf = c_init.astype(BF16)
-    gram_c = gram_local(c_init) / month_total
-    gram_b = total_sum(gram_local(b_init)) / term_total
+    devices = slab_count * grid_count
+    ones = jnp.ones((1, c_init.shape[1]), F32)
     term_panel = lax.all_gather(b_init.astype(BF16), "slab", axis=0, tiled=True)
-    moments_a = block_moments(0, local_blocks, local_coords, filled, term_panel, month_bf, doc_rows)
-    parts_a = exchange(moments_a, "grid")
+    term_panel, b_held = lax.optimization_barrier((term_panel, b_init))
+    gram_c = (gram_local(c_init), month_total, ones)
+    gram_b = (total_sum(gram_local(b_held)), term_total, ones)
+
+    moments_a = block_moments(
+        0, (None, None, "grid"), local_blocks, local_coords, filled, term_panel, month_bf, doc_rows
+    )
+    others_a = swap_pieces(moments_a, "grid")
     inverse_a = product_inverse(gram_b, gram_c)
-    raw_a, own_gram_a = solve_rows(parts_a, inverse_a, True)
-    factor_a, rounded_a, gram_a = scale_rows(total_sum(own_gram_a), raw_a, doc_total)
-    doc_panel = lax.all_gather(rounded_a, "grid", axis=0, tiled=True)
-    moments_b = block_moments(1, local_blocks, local_coords, filled, doc_panel, month_bf, term_rows)
-    parts_b = exchange(moments_b, "slab")
+    raw_a, own_gram_a, squares_a = solve_swapped(moments_a, others_a, inverse_a, devices)
+    all_squares_a = exchange(squares_a, BOTH)[:, 0]
+    factor_a, rounded_a, scale_a = scale_rows(all_squares_a, raw_a, doc_total)
+    doc_panel = swap_gather(rounded_a, "grid")
+    own_gram_a, rounded_a = lax.optimization_barrier((own_gram_a, rounded_a))
+    gram_a = (total_sum(own_gram_a), doc_total, scale_a)
+
+    moments_b = block_moments(
+        1, ("grid", None, "slab"), local_blocks, local_coords, filled, doc_panel, month_bf, term_rows
+    )
+    others_b = swap_pieces(moments_b, "slab")
     inverse_b = product_inverse(gram_a, gram_c)
-    raw_b, own_gram_b = solve_rows(parts_b, inverse_b, True)
-    factor_b, rounded_b, gram_bn = scale_rows(total_sum(own_gram_b), raw_b, term_total)
+    raw_b, own_gram_b, squares_b = solve_swapped(moments_b, others_b, inverse_b, devices)
+    all_squares_b = exchange(squares_b, BOTH)[:, 0]
+    factor_b, rounded_b, scale_b = scale_rows(all_squares_b, raw_b, term_total)
     term_panel_new = lax.all_gather(rounded_b, "slab", axis=0, tiled=True)
+    own_gram_b, rounded_b = lax.optimization_barrier((own_gram_b, rounded_b))
+    gram_bn = (total_sum(own_gram_b), term_total, scale_b)
+
     moments_c = block_moments(
-        2, local_blocks, local_coords, filled, term_panel_new, doc_panel, month_total
+        2, (None, "grid", None), local_blocks, local_coords, filled, term_panel_new, doc_panel, month_total
     )
     parts_c = exchange(moments_c, BOTH)
     inverse_c = product_inverse(gram_a, gram_bn)
-    (raw_own,) = solve_rows(parts_c, inverse_c, False)
-    raw_c = spread_rows(raw_own, BOTH)
+    raw_c = spread_rows(solve_stacked(parts_c, inverse_c), BOTH)
     column_scale = jnp.sqrt(jnp.mean(raw_c * raw_c, axis=0) + EPS)
     return (factor_a, factor_b, raw_c / column_scale)
 

time: 240 us -> 240 us (level); the launches traced: 242 us -> 237 us
  blocking collectives: 127 us -> 71.9 us
  starting transfers between devices: 20.7 us -> 53.3 us
  waiting for transfers between devices: 20 us -> 35.6 us
    ppermute x0 -> x13, waiting for transfers between devices: none -> 27.9 us  [swap(): lax.ppermute(rows, axis, [(i, i ^ step) for i in range(lax.axis_size(axis...]
    ppermute x0 -> x13, starting transfers between devices: none -> 26 us  [swap(): lax.ppermute(rows, axis, [(i, i ^ step) for i in range(lax.axis_size(axis...]
    all_to_all x3 -> x1, blocking collectives: 41.1 us -> 15.6 us  [spread_rows(): lax.all_to_all(jnp.tile(rows, (devices, 1)), axes, split_axis=0, concat_a...]
    all_gather x1 -> x0, blocking collectives: 16.1 us -> none  [on_device(): doc_panel = lax.all_gather(rounded_a, 'grid', axis=0, tiled=True)]
    all_to_all x3, blocking collectives: 50.5 us -> 34.4 us  [exchange(): parts = lax.all_to_all(rows, axes, split_axis=0, concat_axis=0, tiled=True)]
    all_to_all x3, waiting for transfers between devices: 20 us -> 7.74 us  [exchange(): parts = lax.all_to_all(rows, axes, split_axis=0, concat_axis=0, tiled=True)]
    all_to_all x1 -> x3, starting transfers between devices: 2.72 us -> 9.2 us  [spread_rows(): lax.all_to_all(jnp.tile(rows, (devices, 1)), axes, split_axis=0, concat_a...]
    unnamed x9 -> x14, local copies, waits for them, and re-layouts: 10.9 us -> 10.9 us
  transfers between devices with their start and end apart: 4 -> 19, of which waited for: 2 -> 5; matrix products, arithmetic and copies ran while one was open for 1% -> 1% of each run, Pallas kernels for 15% -> 21%
where the time goes in v1:
time: 240 us; the launch traced here: 237 us
  blocking collectives  71.9 us (30%)
  Pallas kernels  55.3 us (23%)
  starting transfers between devices  53.3 us (22%)
  waiting for transfers between devices  35.6 us (15%)
  local copies, waits for them, and re-layouts  14.1 us (6%)
  other arithmetic  2.83 us (1%)
  matrix products  2.69 us (1%)
    all_to_all x3, blocking collectives, exchange(): parts = lax.all_to_all(rows, axes, split_axis=0, concat_axis=0, tiled=True)  34.4 us
    pallas_call x3, Pallas kernels, product_inverse(): pl.pallas_call(functools.partial(inverse_kernel, (one[1], two[1])), out_s...  32.8 us
    ppermute x13, waiting for transfers between devices, swap(): lax.ppermute(rows, axis, [(i, i ^ step) for i in range(lax.axis_size(axis...  27.9 us
    ppermute x13, starting transfers between devices, swap(): lax.ppermute(rows, axis, [(i, i ^ step) for i in range(lax.axis_size(axis...  26 us
    all_to_all x3, starting transfers between devices, exchange(): parts = lax.all_to_all(rows, axes, split_axis=0, concat_axis=0, tiled=True)  18.2 us
    pallas_call x3, Pallas kernels, block_moments(): pl.pallas_call(functools.partial(moments_kernel, mode, orders), grid_spec...  18.1 us
    all_to_all x1, blocking collectives, spread_rows(): lax.all_to_all(jnp.tile(rows, (devices, 1)), axes, split_axis=0, concat_a...  15.6 us
    all_gather x1, blocking collectives, on_device(): term_panel = lax.all_gather(b_init.astype(BF16), 'slab', axis=0, tiled=True)  11.3 us
  transfers between devices with their start and end apart: 19, of which 5 were waited for; matrix products, arithmetic and copies ran while one was open for 1% of the time, Pallas kernels for 21%

profile of v1, /device:TPU:0, one launch (start us, length us, event | category | flops | bytes accessed | tf_op | source)
XLA Modules:
  0.0 237.4 jit_solution(12276435202384024025)
XLA Ops:
  0.6 0.0 copy-start.3
  0.6 1.0 convert_element_type.6
  1.6 11.3 %all_gather.6.first_ref = bf16[1024,256]{1,0:T(8,128)(2,1)S(1)} all-gather(bf16[128,256]{1,0:T(8,128)(2,1)S(1)} %convert_element_type.6), channel_id=1, replica_groups=mesh['slab'=8,'grid'=4] {'slab'}, dimensions={0}, use_global_device_ids=true | all-gather | bytes 589824 | tf_op jit(solution)/shard_map/all_gather | solution.py:356
  12.9 2.1 convolution_bitcast_fusion
  15.0 4.9 %all-to-all-start = ((f32[32,8,256]{2,1,0:T(8,128)}), f32[32,8,256]{2,1,0:T(8,128)S(1)}, u32[]{:S(2)}, u32[]{:S(2)}) async-start(f32[32,8,256]{2,1,0:T(8,128)} %convolution_bitcast_fusion), calls=%async_computation | async-start | bytes 524288 | tf_op jit(solution)/shard_map/all_to_all | solution.py:136
  20.6 0.8 copy.10
  21.3 0.1 reshape.66.coords_ref
  21.4 1.0 convert_element_type.7.second_ref
  22.4 7.7 %all-to-all-done = f32[32,8,256]{2,1,0:T(8,128)S(1)} async-done(((f32[32,8,256]{2,1,0:T(8,128)}), f32[32,8,256]{2,1,0:T(8,128)S(1)}, u32[]{:S(2)}, u32[]{:S(2)}) %all-to-all-start) | async-done | bytes 262176 | tf_op jit(solution)/shard_map/all_to_all | solution.py:136
  30.2 0.7 tile.8
  30.9 2.7 %all-to-all-start.1 = ((f32[32,8,256]{2,1,0:T(8,128)}), f32[32,8,256]{2,1,0:T(8,128)S(1)}, u32[]{:S(2)}, u32[]{:S(2)}) async-start(f32[32,8,256]{2,1,0:T(8,128)} %tile.8), calls=%async_computation.1 | async-start | bytes 524288 | tf_op jit(solution)/shard_map/all_to_all | solution.py:142
  33.6 0.0 copy-start
  33.6 3.4 %copy-done = bf16[1,1,16,64,4096]{4,3,2,1,0:T(8,128)(2,1)S(1)} copy-done((bf16[1,1,16,64,4096]{4,3,2,1,0:T(8,128)(2,1)S(1)}, bf16[1,1,16,64,4096]{4,3,2,1,0:T(8,128)(2,1)}, u32[]{:S(2)}) %copy-start) | copy-done | bytes 8388632
  37.0 4.0 %shard_map.76.refs_0_ = f32[1024,256]{1,0:T(8,128)S(1)} custom-call(s32[1]{0:T(128)} %bitcast.26.count_ref, s32[48]{0:T(128)S(1)} %reshape.66.coords_ref, bf16[16,64,4096]{2,1,0:T(8,128)(2,1)S(1)} %bitcast.29, bf16[1024,256]{1,0:T(8,128)(2,1)S(1)} %all_gather.6.first_ref, bf16[256,256]{1,0:T(8,128)(2,1)S(1)} %convert_element_type.7.second_ref), custom_call_target="tpu_custom_call" | custom-call | flops 2147483648 | bytes 8388608 | tf_op jit(solution)/shard_map/pallas_call | solution.py:123
  41.0 0.1 fusion.1
  41.0 3.2 %collective-permute-start.2 = (f32[256,256]{1,0:T(8,128)S(1)}, f32[256,256]{1,0:T(8,128)S(1)}, u32[]{:S(2)}, u32[]{:S(2)}) collective-permute-start(f32[256,256]{1,0:T(8,128)S(1)} %get-tuple-element.42), channel_id=1, source_target_pairs={{0,3},{1,2},{2,1},{3,0},{4,7},{5,6},{6,5},{7,4},{8,11},{9,10},{10,... | collective-permute-start | bytes 786440 | tf_op jit(solution)/shard_map/ppermute | solution.py:150
  44.2 0.6 collective-permute-start.1
  44.8 0.7 collective-permute-start
  45.5 0.6 fusion.2.two_ref
  46.1 10.9 %shard_map.77.refs_4_ = f32[256,256]{1,0:T(8,128)S(1)} custom-call(f32[256,256]{1,0:T(8,128)S(1)} %bitcast.34, f32[1,256]{1,0:T(1,128)S(1)} %broadcast_in_dim.4.one_scale_ref.two_scale_ref, f32[256,256]{1,0:T(8,128)S(1)} %fusion.2.two_ref, f32[1,256]{1,0:T(1,128)S(1)} %broadcast_in_dim.4.one_scale_ref.two_scale_ref), custom_call_target="tpu_custom_call" | custom-call | flops 10000000000 | bytes 786432 | tf_op jit(solution)/shard_map/pallas_call | solution.py:274
  57.1 10.0 %collective-permute-done.1.refs_2_ = f32[256,256]{1,0:T(8,128)S(1)} collective-permute-done((f32[256,256]{1,0:T(8,128)S(1)}, f32[256,256]{1,0:T(8,128)S(1)}, u32[]{:S(2)}, u32[]{:S(2)}) %collective-permute-start.1) | collective-permute-done | bytes 262176 | tf_op jit(solution)/shard_map/ppermute | solution.py:150
  67.0 0.0 collective-permute-done.refs_1_
  67.0 1.8 shard_map.78
  68.9 11.9 %all_to_all.91 = f32[32,1,256]{2,1,0:T(1,128)S(1)} all-to-all(f32[32,1,256]{2,1,0:T(1,128)S(1)} %copy.11), channel_id=1, replica_groups=mesh['slab'=8,'grid'=4] {'slab','grid'}, dimensions={0} | all-to-all | bytes 65536 | tf_op jit(solution)/shard_map/all_to_all | solution.py:136
  80.8 0.8 shard_map.79
  81.6 2.6 %all-to-all-start.3 = ((f32[32,8,256]{2,1,0:T(8,128)}), f32[32,8,256]{2,1,0:T(8,128)S(1)}, u32[]{:S(2)}, u32[]{:S(2)}) async-start(f32[32,8,256]{2,1,0:T(8,128)} %bitcast.5), calls=%async_computation.3 | async-start | bytes 524288 | tf_op jit(solution)/shard_map/all_to_all | solution.py:136
  84.2 1.8 collective-permute-start.3
  85.9 2.4 %collective-permute-start.5 = (bf16[256,256]{1,0:T(8,128)(2,1)S(1)}, bf16[256,256]{1,0:T(8,128)(2,1)S(1)}, u32[]{:S(2)}, u32[]{:S(2)}) collective-permute-start(bf16[256,256]{1,0:T(8,128)(2,1)S(1)} %get-tuple-element.24), channel_id=1, source_target_pairs={{0,3},{1,2},{2,1},{3,0},{4,7},{5,6},{6,5},{7,4},{8,11},{9,10},{10,... | collective-permute-start | bytes 393224 | tf_op jit(solution)/shard_map/ppermute | solution.py:150
  88.4 0.1 collective-permute-start.4
  88.4 5.5 %collective-permute-done.3 = bf16[256,256]{1,0:T(8,128)(2,1)S(1)} collective-permute-done((bf16[256,256]{1,0:T(8,128)(2,1)S(1)}, bf16[256,256]{1,0:T(8,128)(2,1)S(1)}, u32[]{:S(2)}, u32[]{:S(2)}) %collective-permute-start.3) | collective-permute-done | bytes 131104 | tf_op jit(solution)/shard_map/ppermute | solution.py:150
  94.0 10.8 %collective-permute-done.4 = bf16[256,256]{1,0:T(8,128)(2,1)S(1)} collective-permute-done((bf16[256,256]{1,0:T(8,128)(2,1)S(1)}, bf16[256,256]{1,0:T(8,128)(2,1)S(1)}, u32[]{:S(2)}, u32[]{:S(2)}) %collective-permute-start.4) | collective-permute-done | bytes 131104 | tf_op jit(solution)/shard_map/ppermute | solution.py:150
  104.8 0.0 collective-permute-done.5
  104.8 0.0 all-to-all-done.3
  104.9 0.7 tile.9
  105.6 3.8 %all-to-all-start.4 = ((f32[32,8,256]{2,1,0:T(8,128)}), f32[32,8,256]{2,1,0:T(8,128)S(1)}, u32[]{:S(2)}, u32[]{:S(2)}) async-start(f32[32,8,256]{2,1,0:T(8,128)} %tile.9), calls=%async_computation.4 | async-start | bytes 524288 | tf_op jit(solution)/shard_map/all_to_all | solution.py:142
  109.4 0.0 copy-start.1
  109.4 3.4 %copy-done.1 = bf16[1,1,16,64,4096]{4,3,2,1,0:T(8,128)(2,1)S(1)} copy-done((bf16[1,1,16,64,4096]{4,3,2,1,0:T(8,128)(2,1)S(1)}, bf16[1,1,16,64,4096]{4,3,2,1,0:T(8,128)(2,1)}, u32[]{:S(2)}) %copy-start.1) | copy-done | bytes 8388632
  112.8 7.4 %shard_map.80.refs_0_ = f32[1024,256]{1,0:T(8,128)S(1)} custom-call(s32[1]{0:T(128)} %bitcast.27.count_ref, s32[48]{0:T(128)S(1)} %reshape.66.coords_ref, bf16[16,64,4096]{2,1,0:T(8,128)(2,1)S(1)} %bitcast.30, bf16[1024,256]{1,0:T(8,128)(2,1)S(1)} %constant_dynamic-update-slice_fusion.first_ref.second_ref, bf16[256,256]{1,0:T(8,128)(2,1)S(1)} %convert_element_type.7.second_ref), custom_call_target="tpu_custom_call" | custom-call | flops 2147483648 | bytes 8388608 | tf_op jit(solution)/shard_map/pallas_call | solution.py:123
  120.2 0.7 fusion
  120.9 13.2 %collective-permute-start.11 = (f32[128,256]{1,0:T(8,128)S(1)}, f32[128,256]{1,0:T(8,128)S(1)}, u32[]{:S(2)}, u32[]{:S(2)}) collective-permute-start(f32[128,256]{1,0:T(8,128)S(1)} %get-tuple-element.36), channel_id=1, source_target_pairs={{0,24},{4,28},{8,16},{12,20},{16,8},{20,12},{24,0},{28,4},{1,25},{... | collective-permute-start | bytes 393224 | tf_op jit(solution)/shard_map/ppermute | solution.py:150
  134.1 1.7 collective-permute-start.9
  135.8 0.9 collective-permute-start.8
  136.7 0.9 collective-permute-start.7
  137.6 1.6 collective-permute-done.11.refs_6_
  139.2 0.6 collective-permute-start.6
  139.8 10.9 %shard_map.81.refs_8_ = f32[256,256]{1,0:T(8,128)S(1)} custom-call(f32[256,256]{1,0:T(8,128)S(1)} %bitcast.32, f32[1,256]{1,0:T(1,128)S(1)} %get-tuple-element.27.one_scale_ref, f32[256,256]{1,0:T(8,128)S(1)} %fusion.2.two_ref, f32[1,256]{1,0:T(1,128)S(1)} %broadcast_in_dim.4.one_scale_ref.two_scale_ref), custom_call_target="tpu_custom_call" | custom-call | flops 10000000000 | bytes 786432 | tf_op jit(solution)/shard_map/pallas_call | solution.py:274
  150.7 0.0 collective-permute-done.10.refs_5_
  150.7 0.0 collective-permute-done.8.refs_3_
  150.8 0.0 collective-permute-done.7.refs_2_
  150.8 0.9 shard_map.82
  151.7 10.6 %all_to_all.92 = f32[32,1,256]{2,1,0:T(1,128)S(1)} all-to-all(f32[32,1,256]{2,1,0:T(1,128)S(1)} %copy.12), channel_id=1, replica_groups=mesh['slab'=8,'grid'=4] {'slab','grid'}, dimensions={0} | all-to-all | bytes 65536 | tf_op jit(solution)/shard_map/all_to_all | solution.py:136
  162.3 0.7 shard_map.83
  163.0 11.9 %all_to_all.93 = f32[32,8,256]{2,1,0:T(8,128)S(1)} all-to-all(f32[32,8,256]{2,1,0:T(8,128)S(1)} %bitcast.36), channel_id=1, replica_groups=mesh['slab'=8,'grid'=4] {'slab','grid'}, dimensions={0} | all-to-all | bytes 524288 | tf_op jit(solution)/shard_map/all_to_all | solution.py:136
  174.9 0.7 tile.10
  175.6 2.7 %all-to-all-start.8 = ((f32[32,8,256]{2,1,0:T(8,128)}), f32[32,8,256]{2,1,0:T(8,128)S(1)}, u32[]{:S(2)}, u32[]{:S(2)}) async-start(f32[32,8,256]{2,1,0:T(8,128)} %tile.10), calls=%async_computation.8 | async-start | bytes 524288 | tf_op jit(solution)/shard_map/all_to_all | solution.py:142
  178.3 10.6 %all_gather.7.first_ref = bf16[1024,256]{1,0:T(8,128)(2,1)S(1)} all-gather(bf16[128,256]{1,0:T(8,128)(2,1)S(1)} %get-tuple-element.31), channel_id=1, replica_groups=mesh['slab'=8,'grid'=4] {'slab'}, dimensions={0}, use_global_device_ids=true | all-gather | bytes 589824 | tf_op jit(solution)/shard_map/all_gather | solution.py:381
  188.9 3.4 %copy-done.2 = bf16[1,1,16,64,4096]{4,3,2,1,0:T(8,128)(2,1)S(1)} copy-done((bf16[1,1,16,64,4096]{4,3,2,1,0:T(8,128)(2,1)S(1)}, bf16[1,1,16,64,4096]{4,3,2,1,0:T(8,128)(2,1)}, u32[]{:S(2)}) %copy-start.2) | copy-done | bytes 8388632
  192.3 6.8 %shard_map.84 = f32[256,256]{1,0:T(8,128)} custom-call(s32[1]{0:T(128)} %bitcast.28.count_ref, s32[48]{0:T(128)S(1)} %reshape.66.coords_ref, bf16[16,64,4096]{2,1,0:T(8,128)(2,1)S(1)} %bitcast.31, bf16[1024,256]{1,0:T(8,128)(2,1)S(1)} %all_gather.7.first_ref, bf16[1024,256]{1,0:T(8,128)(2,1)S(1)} %constant_dynamic-update-slice_fusion.first_ref.second_ref), custom_call_target="tpu_custom_call" | custom-call | flops 2147483648 | bytes 8388608 | tf_op jit(solution)/shard_map/pallas_call | solution.py:123
  199.1 10.7 %all-to-all-start.6 = ((f32[32,8,256]{2,1,0:T(8,128)}), f32[32,8,256]{2,1,0:T(8,128)S(1)}, u32[]{:S(2)}, u32[]{:S(2)}) async-start(f32[32,8,256]{2,1,0:T(8,128)} %bitcast.8), calls=%async_computation.6 | async-start | bytes 524288 | tf_op jit(solution)/shard_map/all_to_all | solution.py:136
  209.7 10.9 %shard_map.85.refs_1_ = f32[256,256]{1,0:T(8,128)S(1)} custom-call(f32[256,256]{1,0:T(8,128)S(1)} %bitcast.33, f32[1,256]{1,0:T(1,128)S(1)} %get-tuple-element.27.one_scale_ref, f32[256,256]{1,0:T(8,128)S(1)} %bitcast.35, f32[1,256]{1,0:T(1,128)S(1)} %get-tuple-element.34.two_scale_ref), custom_call_target="tpu_custom_call" | custom-call | flops 10000000000 | bytes 786432 | tf_op jit(solution)/shard_map/pallas_call | solution.py:274
  220.7 0.0 all-to-all-done.6.refs_0_
  220.7 0.2 shard_map.86
  221.0 15.6 %all_to_all.94 = f32[32,8,256]{2,1,0:T(8,128)S(1)} all-to-all(f32[32,8,256]{2,1,0:T(8,128)S(1)} %tile.11), channel_id=1, replica_groups=mesh['slab'=8,'grid'=4] {'slab','grid'}, dimensions={0} | all-to-all | bytes 524288 | tf_op jit(solution)/shard_map/all_to_all | solution.py:142
  236.7 0.7 bitcast_divide_fusion
  (26 shorter events, 0.3 us)
Async XLA Ops:
  0.6 44.8 %copy-start.3 = (f32[256,256]{1,0:T(8,128)S(1)}, f32[256,256]{1,0:T(8,128)}, u32[]{:S(2)}) copy-start(f32[256,256]{1,0:T(8,128)} %param.9) | copy-start | bytes 786436
  15.0 15.1 %all-to-all-start = ((f32[32,8,256]{2,1,0:T(8,128)}), f32[32,8,256]{2,1,0:T(8,128)S(1)}, u32[]{:S(2)}, u32[]{:S(2)}) async-start(f32[32,8,256]{2,1,0:T(8,128)} %convolution_bitcast_fusion), calls=%async_computation | async-start | bytes 524288 | tf_op jit(solution)/shard_map/all_to_all | solution.py:136
  30.9 15.2 %all-to-all-start.1 = ((f32[32,8,256]{2,1,0:T(8,128)}), f32[32,8,256]{2,1,0:T(8,128)S(1)}, u32[]{:S(2)}, u32[]{:S(2)}) async-start(f32[32,8,256]{2,1,0:T(8,128)} %tile.8), calls=%async_computation.1 | async-start | bytes 524288 | tf_op jit(solution)/shard_map/all_to_all | solution.py:142
  33.6 3.4 %copy-start = (bf16[1,1,16,64,4096]{4,3,2,1,0:T(8,128)(2,1)S(1)}, bf16[1,1,16,64,4096]{4,3,2,1,0:T(8,128)(2,1)}, u32[]{:S(2)}) copy-start(bf16[1,1,16,64,4096]{4,3,2,1,0:T(8,128)(2,1)} %param.5) | copy-start | bytes 25165828
  41.0 16.0 %collective-permute-start.2 = (f32[256,256]{1,0:T(8,128)S(1)}, f32[256,256]{1,0:T(8,128)S(1)}, u32[]{:S(2)}, u32[]{:S(2)}) collective-permute-start(f32[256,256]{1,0:T(8,128)S(1)} %get-tuple-element.42), channel_id=1, source_target_pairs={{0,3},{1,2},{2,1},{3,0},{4,7},{5,6},{6,5},{7,4},{8,11},{9,10},{10,... | collective-permute-start | bytes 786440 | tf_op jit(solution)/shard_map/ppermute | solution.py:150
  44.2 22.8 %collective-permute-start.1 = (f32[256,256]{1,0:T(8,128)S(1)}, f32[256,256]{1,0:T(8,128)S(1)}, u32[]{:S(2)}, u32[]{:S(2)}) collective-permute-start(f32[256,256]{1,0:T(8,128)S(1)} %get-tuple-element.43), channel_id=1, source_target_pairs={{0,2},{1,3},{2,0},{3,1},{4,6},{5,7},{6,4},{7,5},{8,10},{9,11},{10,... | collective-permute-start | bytes 786440 | tf_op jit(solution)/shard_map/ppermute | solution.py:150
  44.8 22.2 %collective-permute-start = (f32[256,256]{1,0:T(8,128)S(1)}, f32[256,256]{1,0:T(8,128)S(1)}, u32[]{:S(2)}, u32[]{:S(2)}) collective-permute-start(f32[256,256]{1,0:T(8,128)S(1)} %get-tuple-element.44), channel_id=1, source_target_pairs={{0,1},{1,0},{2,3},{3,2},{4,5},{5,4},{6,7},{7,6},{8,9},{9,8},{10,11... | collective-permute-start | bytes 786440 | tf_op jit(solution)/shard_map/ppermute | solution.py:150
  81.6 23.2 %all-to-all-start.3 = ((f32[32,8,256]{2,1,0:T(8,128)}), f32[32,8,256]{2,1,0:T(8,128)S(1)}, u32[]{:S(2)}, u32[]{:S(2)}) async-start(f32[32,8,256]{2,1,0:T(8,128)} %bitcast.5), calls=%async_computation.3 | async-start | bytes 524288 | tf_op jit(solution)/shard_map/all_to_all | solution.py:136
  84.2 9.8 %collective-permute-start.3 = (bf16[256,256]{1,0:T(8,128)(2,1)S(1)}, bf16[256,256]{1,0:T(8,128)(2,1)S(1)}, u32[]{:S(2)}, u32[]{:S(2)}) collective-permute-start(bf16[256,256]{1,0:T(8,128)(2,1)S(1)} %get-tuple-element.24), channel_id=1, source_target_pairs={{0,1},{1,0},{2,3},{3,2},{4,5},{5,4},{6,7},{7,6},{8,9},{9,8},{10,11... | collective-permute-start | bytes 393224 | tf_op jit(solution)/shard_map/ppermute | solution.py:150
  85.9 18.9 %collective-permute-start.5 = (bf16[256,256]{1,0:T(8,128)(2,1)S(1)}, bf16[256,256]{1,0:T(8,128)(2,1)S(1)}, u32[]{:S(2)}, u32[]{:S(2)}) collective-permute-start(bf16[256,256]{1,0:T(8,128)(2,1)S(1)} %get-tuple-element.24), channel_id=1, source_target_pairs={{0,3},{1,2},{2,1},{3,0},{4,7},{5,6},{6,5},{7,4},{8,11},{9,10},{10,... | collective-permute-start | bytes 393224 | tf_op jit(solution)/shard_map/ppermute | solution.py:150
  88.4 16.4 %collective-permute-start.4 = (bf16[256,256]{1,0:T(8,128)(2,1)S(1)}, bf16[256,256]{1,0:T(8,128)(2,1)S(1)}, u32[]{:S(2)}, u32[]{:S(2)}) collective-permute-start(bf16[256,256]{1,0:T(8,128)(2,1)S(1)} %get-tuple-element.24), channel_id=1, source_target_pairs={{0,2},{1,3},{2,0},{3,1},{4,6},{5,7},{6,4},{7,5},{8,10},{9,11},{10,... | collective-permute-start | bytes 393224 | tf_op jit(solution)/shard_map/ppermute | solution.py:150
  105.6 34.2 %all-to-all-start.4 = ((f32[32,8,256]{2,1,0:T(8,128)}), f32[32,8,256]{2,1,0:T(8,128)S(1)}, u32[]{:S(2)}, u32[]{:S(2)}) async-start(f32[32,8,256]{2,1,0:T(8,128)} %tile.9), calls=%async_computation.4 | async-start | bytes 524288 | tf_op jit(solution)/shard_map/all_to_all | solution.py:142
  109.4 3.4 %copy-start.1 = (bf16[1,1,16,64,4096]{4,3,2,1,0:T(8,128)(2,1)S(1)}, bf16[1,1,16,64,4096]{4,3,2,1,0:T(8,128)(2,1)}, u32[]{:S(2)}) copy-start(bf16[1,1,16,64,4096]{4,3,2,1,0:T(8,128)(2,1)} %param.5) | copy-start | bytes 25165828
  120.9 15.8 %collective-permute-start.12 = (f32[128,256]{1,0:T(8,128)S(1)}, f32[128,256]{1,0:T(8,128)S(1)}, u32[]{:S(2)}, u32[]{:S(2)}) collective-permute-start(f32[128,256]{1,0:T(8,128)S(1)} %get-tuple-element.35), channel_id=1, source_target_pairs={{0,28},{4,24},{8,20},{12,16},{16,12},{20,8},{24,4},{28,0},{1,29},{... | collective-permute-start | bytes 393224 | tf_op jit(solution)/shard_map/ppermute | solution.py:150
  120.9 18.3 %collective-permute-start.11 = (f32[128,256]{1,0:T(8,128)S(1)}, f32[128,256]{1,0:T(8,128)S(1)}, u32[]{:S(2)}, u32[]{:S(2)}) collective-permute-start(f32[128,256]{1,0:T(8,128)S(1)} %get-tuple-element.36), channel_id=1, source_target_pairs={{0,24},{4,28},{8,16},{12,20},{16,8},{20,12},{24,0},{28,4},{1,25},{... | collective-permute-start | bytes 393224 | tf_op jit(solution)/shard_map/ppermute | solution.py:150
  134.1 16.7 %collective-permute-start.10 = (f32[128,256]{1,0:T(8,128)}, f32[128,256]{1,0:T(8,128)S(1)}, u32[]{:S(2)}, u32[]{:S(2)}) collective-permute-start(f32[128,256]{1,0:T(8,128)} %get-tuple-element.37), channel_id=1, source_target_pairs={{0,20},{4,16},{8,28},{12,24},{16,4},{20,0},{24,12},{28,8},{1,21},{... | collective-permute-start | bytes 393224 | tf_op jit(solution)/shard_map/ppermute | solution.py:150
  134.1 16.7 %collective-permute-start.9 = (f32[128,256]{1,0:T(8,128)S(1)}, f32[128,256]{1,0:T(8,128)S(1)}, u32[]{:S(2)}, u32[]{:S(2)}) collective-permute-start(f32[128,256]{1,0:T(8,128)S(1)} %get-tuple-element.38), channel_id=1, source_target_pairs={{0,16},{4,20},{8,24},{12,28},{16,0},{20,4},{24,8},{28,12},{1,17},{... | collective-permute-start | bytes 393224 | tf_op jit(solution)/shard_map/ppermute | solution.py:150
  135.8 15.0 %collective-permute-start.8 = (f32[128,256]{1,0:T(8,128)S(1)}, f32[128,256]{1,0:T(8,128)S(1)}, u32[]{:S(2)}, u32[]{:S(2)}) collective-permute-start(f32[128,256]{1,0:T(8,128)S(1)} %get-tuple-element.39), channel_id=1, source_target_pairs={{0,12},{4,8},{8,4},{12,0},{16,28},{20,24},{24,20},{28,16},{1,13},{... | collective-permute-start | bytes 393224 | tf_op jit(solution)/shard_map/ppermute | solution.py:150
  136.7 14.0 %collective-permute-start.7 = (f32[128,256]{1,0:T(8,128)S(1)}, f32[128,256]{1,0:T(8,128)S(1)}, u32[]{:S(2)}, u32[]{:S(2)}) collective-permute-start(f32[128,256]{1,0:T(8,128)S(1)} %get-tuple-element.40), channel_id=1, source_target_pairs={{0,8},{4,12},{8,0},{12,4},{16,24},{20,28},{24,16},{28,20},{1,9},{5... | collective-permute-start | bytes 393224 | tf_op jit(solution)/shard_map/ppermute | solution.py:150
  139.2 11.6 %collective-permute-start.6 = (f32[128,256]{1,0:T(8,128)S(1)}, f32[128,256]{1,0:T(8,128)S(1)}, u32[]{:S(2)}, u32[]{:S(2)}) collective-permute-start(f32[128,256]{1,0:T(8,128)S(1)} %get-tuple-element.41), channel_id=1, source_target_pairs={{0,4},{4,0},{8,12},{12,8},{16,20},{20,16},{24,28},{28,24},{1,5},{5... | collective-permute-start | bytes 393224 | tf_op jit(solution)/shard_map/ppermute | solution.py:150
  175.6 23.4 %all-to-all-start.8 = ((f32[32,8,256]{2,1,0:T(8,128)}), f32[32,8,256]{2,1,0:T(8,128)S(1)}, u32[]{:S(2)}, u32[]{:S(2)}) async-start(f32[32,8,256]{2,1,0:T(8,128)} %tile.10), calls=%async_computation.8 | async-start | bytes 524288 | tf_op jit(solution)/shard_map/all_to_all | solution.py:142
  188.9 3.4 %copy-start.2 = (bf16[1,1,16,64,4096]{4,3,2,1,0:T(8,128)(2,1)S(1)}, bf16[1,1,16,64,4096]{4,3,2,1,0:T(8,128)(2,1)}, u32[]{:S(2)}) copy-start(bf16[1,1,16,64,4096]{4,3,2,1,0:T(8,128)(2,1)} %param.5) | copy-start | bytes 25165828
  199.1 21.6 %all-to-all-start.6 = ((f32[32,8,256]{2,1,0:T(8,128)}), f32[32,8,256]{2,1,0:T(8,128)S(1)}, u32[]{:S(2)}, u32[]{:S(2)}) async-start(f32[32,8,256]{2,1,0:T(8,128)} %bitcast.8), calls=%async_computation.6 | async-start | bytes 524288 | tf_op jit(solution)/shard_map/all_to_all | solution.py:136
